TPU v7x, 256 devices: a whole 4x4x8 slice. The times are simulated.
256 devices in a mesh: ckpt: 4 (over z_lo), tok: 64 (over y, z_hi, x, core).
Axes of the slice: x: 4, y: 4, z: 8 (z_hi: 2, z_lo: 4; z = z_hi * 4 + z_lo), core: 2. Of those that a mesh axis runs over, the one named last changes fastest.
Arguments:
- features: bfloat16 [4, 8192, 1792], P('ckpt', 'tok'), may hold values from -22 to 22
- pairing: int32 [4, 64, 128], P('ckpt', 'tok'), may hold values from 0 to 127, each once within a row
- rotation: bfloat16 [4, 1792, 1792], P('ckpt', 'tok'), may hold values from -1 to 2
Outputs:
- consensus: bfloat16 [8192, 1792], P('tok')
- rotation_next: bfloat16 [4, 1792, 1792], P('ckpt', 'tok')
Inputs may be any that keep to these rules, and one draw needn't show every extreme that they name: Each row of a shard of 128 rows appears once in that shard's pairing.
All inputs are finite; a program needn't handle non-finite values.
Results may differ from a plain program's by a relative error of at most 0.011.
Values may be sent and summed in bfloat16 or wider, within the bound.
A program may use at most 64 MiB of HBM per device.

v0:
```python
import math
import jax
import jax.numpy as jnp
from jax import lax
from jax.sharding import PartitionSpec as P


def apply_once(vector, whole):
    inner = lax.dot_general(
        vector.astype(jnp.bfloat16),
        whole,
        (((1,), (1,)), ((), ())),
        preferred_element_type=jnp.float32,
    ).astype(jnp.bfloat16)
    return jnp.dot(inner, whole, preferred_element_type=jnp.float32)


def normalize(own_cov, feature_width):
    squares = lax.psum(jnp.sum(own_cov * own_cov), "tok")
    return (own_cov / (2.0 * jnp.sqrt(squares / feature_width + 1e-06))).astype(jnp.bfloat16)


def block_form(aligned, consensus, devices, column_groups, send_fn, collect_fn):
    row_count, feature_width = aligned.shape
    row_groups = devices // column_groups
    row_width = feature_width // row_groups
    col_width = feature_width // column_groups
    aligned_cols = jnp.repeat(
        aligned.reshape(row_count, row_groups, row_width).transpose(1, 0, 2), column_groups, axis=0
    ).reshape(devices * row_count, row_width)
    consensus_cols = jnp.tile(
        consensus.reshape(row_count, column_groups, col_width).transpose(1, 0, 2),
        (row_groups, 1, 1),
    ).reshape(devices * row_count, col_width)
    aligned_all, consensus_all = send_fn(aligned_cols, consensus_cols)
    own_cov = lax.dot_general(
        aligned_all, consensus_all, (((0,), (0,)), ((), ())), preferred_element_type=jnp.float32
    )
    start_block = normalize(own_cov, feature_width)
    pieces = collect_fn(start_block)
    return (
        pieces.reshape(row_groups, column_groups, row_width, col_width)
        .transpose(0, 2, 1, 3)
        .reshape(feature_width, feature_width)
    )


def shards(features, pairing, rotation):
    own_rows = features[0]
    own_order = pairing[0, 0]
    rot_rows = rotation[0]
    feature_width = own_rows.shape[1]
    aligned = jnp.take(own_rows, own_order, axis=0)
    rotated = jnp.dot(
        aligned,
        lax.all_gather(rot_rows, "tok", axis=0, tiled=True),
        preferred_element_type=jnp.float32,
    ).astype(jnp.bfloat16)
    summed = lax.psum(rotated.astype(jnp.float32).astype(jnp.bfloat16), "ckpt").astype(jnp.float32)
    consensus = (summed / lax.axis_size("ckpt")).astype(jnp.bfloat16)
    devices = lax.axis_size("tok")
    slab_rows = feature_width // devices

    def send_narrow(left, right):
        return (
            lax.all_to_all(left, "tok", split_axis=0, concat_axis=0, tiled=True),
            lax.all_to_all(right, "tok", split_axis=0, concat_axis=0, tiled=True),
        )

    def collect_narrow(block):
        return lax.all_gather(block, "tok", axis=0, tiled=True)

    whole = block_form(aligned, consensus, devices, min(devices, 8), send_narrow, collect_narrow)
    start_rows = lax.dynamic_slice_in_dim(whole, lax.axis_index("tok") * slab_rows, slab_rows, 0)
    first = 1.5 * start_rows.astype(jnp.float32) - 0.5 * apply_once(start_rows, whole)
    upper = 1.5 * first - 0.5 * apply_once(first, whole)
    middle = apply_once(upper, whole)
    cubic = 1.5 * middle - 0.5 * apply_once(middle, whole)
    rotation_next = (math.sqrt(feature_width) * (1.5 * first - 0.5 * cubic)).astype(jnp.bfloat16)
    return (consensus, rotation_next[None])


def solution(mesh):
    placed = (P("ckpt", "tok", None), P("ckpt", "tok", None), P("ckpt", "tok", None))
    return jax.shard_map(
        shards,
        mesh=mesh,
        in_specs=placed,
        out_specs=(P("tok", None), P("ckpt", "tok", None)),
        check_vma=False,
    )
```

profile of v0, /device:TPU:1, one launch (start us, length us, event | category | flops | bytes accessed | tf_op | source)
XLA Modules:
  0.0 733.9 jit_solution(13692629428495231626)
XLA Ops:
  7.2 0.0 copy-start
  7.2 0.0 all-gather.6.cloned.1.call-start
  7.2 1.8 copy.15
  9.0 0.0 all-gather.6.cloned.1.call-update
  9.0 0.7 fusion.25
  9.7 0.0 copy-done
  9.7 0.9 gather_fusion
  10.6 0.3 copy.16
  10.9 0.7 compare_and_fusion
  11.6 2.4 broadcast_in_dim.24
  14.0 15.8 %all-to-all-start = ((bf16[64,128,224]{1,2,0:T(8,128)(2,1)}), bf16[64,128,224]{1,2,0:T(8,128)(2,1)}, u32[]{:S(2)}, u32[]{:S(2)}) async-start(bf16[64,128,224]{1,2,0:T(8,128)(2,1)} %bitcast.41), calls=%async_computation | async-start | bytes 7340032 | tf_op jit(solution)/shard_map/all_to_all | solution.py:66
  29.7 0.0 all-reduce.2.cloned.1.call-start
  29.8 180.5 %all-gather.6.cloned.1.call-done = bf16[1,1792,1792]{2,0,1:T(2,128)(2,1)} async-done(((bf16[1,28,1792]{2,0,1:T(2,128)(2,1)}), bf16[1,1792,1792]{2,0,1:T(2,128)(2,1)}) %all-gather.6.cloned.1.call-update) | async-done | bytes 6422544 | tf_op jit(solution)/shard_map/all_gather | solution.py:56
  210.3 6.5 fusion.3
  216.8 0.0 all-reduce.2.cloned.1.call-update
  216.8 0.0 all-gather.4.cloned.1.call-start
  216.9 43.3 %all-reduce.2.cloned.1.call-done = bf16[128,1792]{1,0:T(8,128)(2,1)} async-done(((bf16[128,1792]{1,0:T(8,128)(2,1)}), bf16[128,1792]{1,0:T(8,128)(2,1)}) %all-reduce.2.cloned.1.call-update) | async-done | bytes 458768 | tf_op jit(solution)/shard_map/psum | solution.py:59
  260.2 1.1 multiply_convert_fusion
  261.3 0.0 copy-start.1
  261.3 0.3 copy.17
  261.5 0.0 all-to-all-done
  261.5 0.6 tile.8
  262.1 96.3 %all_to_all.15 = bf16[64,128,224]{1,2,0:T(8,128)(2,1)S(1)} all-to-all(bf16[64,128,224]{1,2,0:T(8,128)(2,1)S(1)} %bitcast.42), channel_id=1, replica_groups=mesh['ckpt'=4,'tok'=64] {'tok'}, dimensions={0} | all-to-all | bytes 7340032 | tf_op jit(solution)/shard_map/all_to_all | solution.py:67
  358.4 3.8 multiply_reduce_fusion
  362.2 0.0 copy-done.1
  362.2 191.2 %psum.15 = f32[]{:T(128)} all-reduce(f32[]{:T(128)} %get-tuple-element.2), channel_id=1, replica_groups=mesh['ckpt'=4,'tok'=64] {'tok'}, use_global_device_ids=true, to_apply=%region_2.3 | all-reduce | flops 1 | bytes 8 | tf_op jit(solution)/shard_map/psum | solution.py:19
  554.1 0.7 divide_convert_fusion
  554.8 0.0 all-gather.4.cloned.1.call-update
  554.8 117.2 %all-gather.4.cloned.1.call-done = bf16[14336,224]{1,0:T(8,128)(2,1)} async-done(((bf16[224,224]{1,0:T(8,128)(2,1)}), bf16[14336,224]{1,0:T(8,128)(2,1)}) %all-gather.4.cloned.1.call-update) | async-done | bytes 6422544 | tf_op jit(solution)/shard_map/all_gather | solution.py:71
  672.0 10.5 %copy.18 = bf16[8,224,8,224]{3,2,1,0:T(8,128)(2,1)} copy(bf16[8,224,8,224]{3,1,2,0:T(8,128)(2,1)} %bitcast.43) | data formatting | bytes 12845056 | tf_op jit(solution)/shard_map/transpose | solution.py:43
  682.5 13.7 %reshape.66 = bf16[1792,1792]{1,0:T(8,128)(2,1)} reshape(bf16[8,224,8,224]{3,2,1,0:T(8,128)(2,1)} %copy.18) | data formatting | bytes 12845056 | tf_op jit(solution)/shard_map/reshape | solution.py:44
  696.3 7.7 %fusion.10 = f32[28,1792]{1,0:T(8,128)S(1)} fusion(bf16[1792,1792]{1,0:T(8,128)(2,1)} %reshape.66, s32[]{:T(128)S(6)} %select_n.30), kind=kOutput, calls=%fused_computation.12 | convolution fusion | flops 359912448 | bytes 13276160 | tf_op jit(solution)/shard_map/dot_general | solution.py:15
  704.0 7.6 %fusion.12 = bf16[28,1792]{1,0:T(8,128)(2,1)S(1)} fusion(bf16[1792,1792]{1,0:T(8,128)(2,1)} %reshape.66, f32[28,1792]{1,0:T(8,128)S(1)} %fusion.10), kind=kOutput, calls=%fused_computation.14 | convolution fusion | flops 359962624 | bytes 6723584 | tf_op jit(solution)/shard_map/dot_general | solution.py:15
  711.5 7.6 %fusion.15 = f32[28,1792]{1,0:T(8,128)S(1)} fusion(bf16[1792,1792]{1,0:T(8,128)(2,1)} %reshape.66, bf16[28,1792]{1,0:T(8,128)(2,1)S(1)} %fusion.12), kind=kOutput, calls=%fused_computation.22 | convolution fusion | flops 359711744 | bytes 6723584 | tf_op jit(solution)/shard_map/dot_general | solution.py:15
  719.1 8.2 %fusion.14 = bf16[1,28,1792]{2,1,0:T(8,128)(2,1)} fusion(bf16[1792,1792]{1,0:T(8,128)(2,1)} %reshape.66, f32[28,1792]{1,0:T(8,128)S(1)} %fusion.15, f32[28,1792]{1,0:T(8,128)S(1)} %fusion.10), kind=kOutput, calls=%fused_computation.20 | convolution fusion | flops 360163328 | bytes 6924288 | tf_op jit(solution)/shard_map/dot_general | solution.py:15
  (2 shorter events, 0.1 us)
Async XLA Ops:
  7.2 2.5 copy-start
  7.2 203.1 %all-gather.6.cloned.1.call-start = ((), (), s32[]{:S(2)}) async-start(), calls=%async_computation.4 | async-start | bytes 13045760 | tf_op jit(solution)/shard_map/all_gather | solution.py:56
  14.0 247.6 %all-to-all-start = ((bf16[64,128,224]{1,2,0:T(8,128)(2,1)}), bf16[64,128,224]{1,2,0:T(8,128)(2,1)}, u32[]{:S(2)}, u32[]{:S(2)}) async-start(bf16[64,128,224]{1,2,0:T(8,128)(2,1)} %bitcast.41), calls=%async_computation | async-start | bytes 7340032 | tf_op jit(solution)/shard_map/all_to_all | solution.py:66
  29.7 230.4 %all-reduce.2.cloned.1.call-start = ((), (), s32[]{:S(2)}) async-start(), calls=%async_computation.2 | async-start | bytes 917504 | tf_op jit(solution)/shard_map/psum | solution.py:59
  216.8 455.2 %all-gather.4.cloned.1.call-start = ((), (), s32[]{:S(2)}) async-start(), calls=%async_computation.3 | async-start | bytes 7454720 | tf_op jit(solution)/shard_map/all_gather | solution.py:71
  261.3 101.0 %copy-start.1 = (bf16[128,1792]{1,0:T(8,128)(2,1)}, bf16[128,1792]{1,0:T(8,128)(2,1)S(1)}, u32[]{:S(2)}) copy-start(bf16[128,1792]{1,0:T(8,128)(2,1)S(1)} %multiply_convert_fusion) | copy-start | bytes 1376260
Sparse Core Ops, SparseCore 0:
  12.2 198.0 all-gather.5
  216.9 43.1 all-reduce.1
  555.0 117.0 all-gather.3
where the time goes:
time: 735 us; the launch traced here: 734 us
  waiting for transfers between devices  341 us (46%)
  blocking collectives  288 us (39%)
  matrix products  41.3 us (6%)
  local copies, waits for them, and re-layouts  30.5 us (4%)
  starting transfers between devices  15.9 us (2%)
  between operations  14.5 us (2%)
    psum x1, blocking collectives, normalize(): squares = lax.psum(jnp.sum(own_cov * own_cov), 'tok')  191 us
    all_gather x1, waiting for transfers between devices, shards(): lax.all_gather(rot_rows, 'tok', axis=0, tiled=True)  181 us
    all_gather x1, waiting for transfers between devices, collect_narrow(): return lax.all_gather(block, 'tok', axis=0, tiled=True)  117 us
    all_to_all x1, blocking collectives, send_narrow(): lax.all_to_all(right, 'tok', split_axis=0, concat_axis=0, tiled=True)  96.3 us
    psum x1, waiting for transfers between devices, shards(): lax.psum(rotated.astype(jnp.float32).astype(jnp.bfloat16), 'ckpt')  43.3 us
    dot_general x4, matrix products, apply_once(): return jnp.dot(inner, whole, preferred_element_type=jnp.float32)  31.1 us
    all_to_all x1, starting transfers between devices, send_narrow(): lax.all_to_all(left, 'tok', split_axis=0, concat_axis=0, tiled=True)  15.8 us
  transfers between devices with their start and end apart: 4, of which 3 were waited for; matrix products, arithmetic and copies ran while one was open for 2% of the time, Pallas kernels for 0%

commit v1 on v0

--- a/solution.py
+++ b/solution.py
@@ -53,7 +53,9 @@
     aligned = jnp.take(own_rows, own_order, axis=0)
     rotated = jnp.dot(
         aligned,
-        lax.all_gather(rot_rows, "tok", axis=0, tiled=True),
+        jnp.concatenate(
+            lax.all_to_all(jnp.stack([rot_rows] * lax.axis_size("tok")), "tok", 0, 0), axis=0
+        ),
         preferred_element_type=jnp.float32,
     ).astype(jnp.bfloat16)
     summed = lax.psum(rotated.astype(jnp.float32).astype(jnp.bfloat16), "ckpt").astype(jnp.float32)

time: 735 us -> 792 us (1.078)
  waiting for transfers between devices: 341 us -> 378 us
  local copies, waits for them, and re-layouts: 30.5 us -> 43.2 us
  starting transfers between devices: 15.9 us -> 25.2 us
    all_gather x1 -> x0, waiting for transfers between devices: 181 us -> none  [shards(): lax.all_gather(rot_rows, 'tok', axis=0, tiled=True)]
    all_to_all x0 -> x1, waiting for transfers between devices: none -> 162 us  [shards(): lax.all_to_all(jnp.stack([rot_rows] * lax.axis_size('tok')), 'tok', 0, 0)]
    psum x1, waiting for transfers between devices: 43.3 us -> 99.1 us  [shards(): lax.psum(rotated.astype(jnp.float32).astype(jnp.bfloat16), 'ckpt')]
    all_to_all x0 -> x1, starting transfers between devices: none -> 15.9 us  [shards(): lax.all_to_all(jnp.stack([rot_rows] * lax.axis_size('tok')), 'tok', 0, 0)]
    reshape x0 -> x1, local copies, waits for them, and re-layouts: none -> 9.66 us  [shards(): jnp.concatenate(lax.all_to_all(jnp.stack([rot_rows] * lax.axis_size('tok'...]
where the time goes in v1:
time: 792 us; the launch traced here: 791 us
  waiting for transfers between devices  378 us (48%)
  blocking collectives  288 us (36%)
  local copies, waits for them, and re-layouts  43.2 us (5%)
  matrix products  39.5 us (5%)
  starting transfers between devices  25.2 us (3%)
  between operations  14.8 us (2%)
    psum x1, blocking collectives, normalize(): squares = lax.psum(jnp.sum(own_cov * own_cov), 'tok')  191 us
    all_to_all x1, waiting for transfers between devices, shards(): lax.all_to_all(jnp.stack([rot_rows] * lax.axis_size('tok')), 'tok', 0, 0)  162 us
    all_gather x1, waiting for transfers between devices, collect_narrow(): return lax.all_gather(block, 'tok', axis=0, tiled=True)  117 us
    psum x1, waiting for transfers between devices, shards(): lax.psum(rotated.astype(jnp.float32).astype(jnp.bfloat16), 'ckpt')  99.1 us
    all_to_all x1, blocking collectives, send_narrow(): lax.all_to_all(right, 'tok', split_axis=0, concat_axis=0, tiled=True)  96.3 us
    dot_general x4, matrix products, apply_once(): return jnp.dot(inner, whole, preferred_element_type=jnp.float32)  31.1 us
    all_to_all x1, starting transfers between devices, shards(): lax.all_to_all(jnp.stack([rot_rows] * lax.axis_size('tok')), 'tok', 0, 0)  15.9 us
  transfers between devices with their start and end apart: 4, of which 3 were waited for; matrix products, arithmetic and copies ran while one was open for 2% of the time, Pallas kernels for 0%

profile of v1, /device:TPU:1, one launch (start us, length us, event | category | flops | bytes accessed | tf_op | source)
XLA Modules:
  0.0 790.5 jit_solution(4595633521866731865)
XLA Ops:
  7.2 0.0 copy-start
  7.2 4.9 stack.3
  12.0 0.0 copy-start.2
  12.0 15.9 %all-to-all-start = ((bf16[64,28,1792]{2,1,0:T(8,128)(2,1)}), bf16[64,28,1792]{2,1,0:T(8,128)(2,1)}, u32[]{:S(2)}, u32[]{:S(2)}) async-start(bf16[64,28,1792]{2,1,0:T(8,128)(2,1)} %stack.3), calls=%async_computation | async-start | bytes 14680064 | tf_op jit(solution)/shard_map/all_to_all | solution.py:57
  28.0 0.0 copy-done.2
  28.0 0.0 copy-done
  28.0 0.9 gather_fusion
  28.9 0.3 copy.8
  29.3 162.1 %all-to-all-done = bf16[64,28,1792]{2,1,0:T(8,128)(2,1)} async-done(((bf16[64,28,1792]{2,1,0:T(8,128)(2,1)}), bf16[64,28,1792]{2,1,0:T(8,128)(2,1)}, u32[]{:S(2)}, u32[]{:S(2)}) %all-to-all-start) | async-done | bytes 6422560 | tf_op jit(solution)/shard_map/all_to_all | solution.py:57
  191.4 2.3 broadcast_in_dim.24
  193.7 9.2 %all-to-all-start.1 = ((bf16[64,128,224]{1,2,0:T(8,128)(2,1)}), bf16[64,128,224]{1,2,0:T(8,128)(2,1)}, u32[]{:S(2)}, u32[]{:S(2)}) async-start(bf16[64,128,224]{1,2,0:T(8,128)(2,1)} %bitcast.38), calls=%async_computation.1 | async-start | bytes 7340032 | tf_op jit(solution)/shard_map/all_to_all | solution.py:68
  202.9 0.0 all-reduce.2.cloned.1.call-start
  203.0 9.7 %reshape.68 = bf16[1792,1792]{1,0:T(8,128)(2,1)} reshape(bf16[64,28,1792]{2,1,0:T(8,128)(2,1)} %all-to-all-done) | data formatting | bytes 12845056 | tf_op jit(solution)/shard_map/reshape | solution.py:56
  212.6 4.7 convolution_convert_fusion
  217.3 0.0 all-reduce.2.cloned.1.call-update
  217.3 0.0 all-gather.2.cloned.1.call-start
  217.4 99.1 %all-reduce.2.cloned.1.call-done = bf16[128,1792]{1,0:T(8,128)(2,1)} async-done(((bf16[128,1792]{1,0:T(8,128)(2,1)}), bf16[128,1792]{1,0:T(8,128)(2,1)}) %all-reduce.2.cloned.1.call-update) | async-done | bytes 458768 | tf_op jit(solution)/shard_map/psum | solution.py:61
  316.5 1.1 multiply_convert_fusion
  317.6 0.0 copy-start.1
  317.6 0.3 copy.9
  317.8 0.0 all-to-all-done.1
  317.9 0.6 tile.8
  318.5 96.3 %all_to_all.20 = bf16[64,128,224]{1,2,0:T(8,128)(2,1)S(1)} all-to-all(bf16[64,128,224]{1,2,0:T(8,128)(2,1)S(1)} %bitcast.39), channel_id=1, replica_groups=mesh['ckpt'=4,'tok'=64] {'tok'}, dimensions={0} | all-to-all | bytes 7340032 | tf_op jit(solution)/shard_map/all_to_all | solution.py:69
  414.8 3.8 multiply_reduce_fusion
  418.5 0.0 copy-done.1
  418.5 191.2 %psum.15 = f32[]{:T(128)} all-reduce(f32[]{:T(128)} %get-tuple-element.2), channel_id=1, replica_groups=mesh['ckpt'=4,'tok'=64] {'tok'}, use_global_device_ids=true, to_apply=%region_2.3 | all-reduce | flops 1 | bytes 8 | tf_op jit(solution)/shard_map/psum | solution.py:19
  610.5 0.7 divide_convert_fusion
  611.1 0.0 all-gather.2.cloned.1.call-update
  611.2 117.2 %all-gather.2.cloned.1.call-done = bf16[14336,224]{1,0:T(8,128)(2,1)} async-done(((bf16[224,224]{1,0:T(8,128)(2,1)}), bf16[14336,224]{1,0:T(8,128)(2,1)}) %all-gather.2.cloned.1.call-update) | async-done | bytes 6422544 | tf_op jit(solution)/shard_map/all_gather | solution.py:73
  728.3 10.5 %copy.10 = bf16[8,224,8,224]{3,2,1,0:T(8,128)(2,1)} copy(bf16[8,224,8,224]{3,1,2,0:T(8,128)(2,1)} %bitcast.40) | data formatting | bytes 12845056 | tf_op jit(solution)/shard_map/transpose | solution.py:43
  738.9 13.7 %reshape.71 = bf16[1792,1792]{1,0:T(8,128)(2,1)} reshape(bf16[8,224,8,224]{3,2,1,0:T(8,128)(2,1)} %copy.10) | data formatting | bytes 12845056 | tf_op jit(solution)/shard_map/reshape | solution.py:44
  752.6 7.7 fusion.4
  760.3 7.6 fusion.6
  767.9 7.6 fusion.9
  775.4 8.2 %fusion.8 = bf16[1,28,1792]{2,1,0:T(8,128)(2,1)} fusion(bf16[1792,1792]{1,0:T(8,128)(2,1)} %reshape.71, f32[28,1792]{1,0:T(8,128)S(1)} %fusion.9, f32[28,1792]{1,0:T(8,128)S(1)} %fusion.4), kind=kOutput, calls=%fused_computation.17 | convolution fusion | flops 360163328 | bytes 6924288 | tf_op jit(solution)/shard_map/dot_general | solution.py:15
  (4 shorter events, 0.1 us)
Async XLA Ops:
  7.2 20.8 %copy-start = (bf16[1,128,1792]{2,1,0:T(8,128)(2,1)S(1)}, bf16[1,128,1792]{2,1,0:T(8,128)(2,1)}, u32[]{:S(2)}) copy-start(bf16[1,128,1792]{2,1,0:T(8,128)(2,1)} %param.3) | copy-start | bytes 1376260
  12.0 15.9 %copy-start.2 = (s32[1,1,128]{2,1,0:T(1,128)S(1)}, s32[1,1,128]{2,1,0:T(1,128)}, u32[]{:S(2)}) copy-start(s32[1,1,128]{2,1,0:T(1,128)} %param.4) | copy-start | bytes 1540
  12.0 179.4 %all-to-all-start = ((bf16[64,28,1792]{2,1,0:T(8,128)(2,1)}), bf16[64,28,1792]{2,1,0:T(8,128)(2,1)}, u32[]{:S(2)}, u32[]{:S(2)}) async-start(bf16[64,28,1792]{2,1,0:T(8,128)(2,1)} %stack.3), calls=%async_computation | async-start | bytes 14680064 | tf_op jit(solution)/shard_map/all_to_all | solution.py:57
  193.7 124.1 %all-to-all-start.1 = ((bf16[64,128,224]{1,2,0:T(8,128)(2,1)}), bf16[64,128,224]{1,2,0:T(8,128)(2,1)}, u32[]{:S(2)}, u32[]{:S(2)}) async-start(bf16[64,128,224]{1,2,0:T(8,128)(2,1)} %bitcast.38), calls=%async_computation.1 | async-start | bytes 7340032 | tf_op jit(solution)/shard_map/all_to_all | solution.py:68
  202.9 113.6 %all-reduce.2.cloned.1.call-start = ((), (), s32[]{:S(2)}) async-start(), calls=%async_computation.3 | async-start | bytes 917504 | tf_op jit(solution)/shard_map/psum | solution.py:61
  217.3 511.0 %all-gather.2.cloned.1.call-start = ((), (), s32[]{:S(2)}) async-start(), calls=%async_computation.4 | async-start | bytes 7454720 | tf_op jit(solution)/shard_map/all_gather | solution.py:73
  317.6 101.0 %copy-start.1 = (bf16[128,1792]{1,0:T(8,128)(2,1)}, bf16[128,1792]{1,0:T(8,128)(2,1)S(1)}, u32[]{:S(2)}) copy-start(bf16[128,1792]{1,0:T(8,128)(2,1)S(1)} %multiply_convert_fusion) | copy-start | bytes 1376260
Sparse Core Ops, SparseCore 0:
  217.4 99.0 all-reduce.1
  611.3 117.0 all-gather.1
